TPU v7x, 512 devices: a whole 4x4x16 slice. The times are simulated.
512 devices in a mesh: seq: 64 (over y, z), req: 8 (over x, core).
Axes of the slice: x: 4, y: 4, z: 16, core: 2. Of those that a mesh axis runs over, the one named last changes fastest.
Arguments:
- new_token_queries: bfloat16 [4, 64, 2048], P(None, 'req'), may hold values from -48 to 48
- new_token_keys: bfloat16 [4, 64, 1024], P(None, 'req'), may hold values from -48 to 48
- new_token_values: bfloat16 [4, 64, 1024], P(None, 'req'), may hold values from -6 to 6
- key_cache: bfloat16 [64, 2048, 1024], P('req', 'seq'), may hold values from -48 to 48
- value_cache: bfloat16 [64, 2048, 1024], P('req', 'seq'), may hold values from -6 to 6
- cache_len: int32 [64], P('req'), may hold values from 1 to 2048, 34816 in all
- resid: bfloat16 [4, 64, 2048], P(None, 'req'), may hold values from -6 to 6
- gain: bfloat16 [2048], replicated, may hold values from 0.5 to 1.5
- w_gate: bfloat16 [2048, 6144], P('seq', 'req'), may hold values from -0.125 to 0.125
- w_up: bfloat16 [2048, 6144], P('seq', 'req'), may hold values from -0.125 to 0.125
- w_down: bfloat16 [6144, 2048], P('req', 'seq'), may hold values from -0.078125 to 0.078125
Outputs:
- out: bfloat16 [4, 64, 2048], P(None, 'req')
All inputs are finite; a program needn't handle non-finite values. No bound on the sum of `cache_len` on one device may be relied on, other than what follows from the above.
Results may differ from a plain program's by a relative error of at most 0.006.
Values may be sent and summed in bfloat16 or wider, within the bound.
A program may use at most 128 MiB of HBM per device.

v0:
```python
import math
import jax
import jax.numpy as jnp
from jax import lax
from jax.sharding import PartitionSpec as P

QUERY_HEADS = 16
KEY_VALUE_HEADS = 8
HEAD_SIZE = 128
NEG_FILL = -1e30
EPSILON = 1e-06


def partial_softmax(q, keys, values, valid):
    scores = jnp.einsum("rkmd,rbkd->rkmb", q, keys, preferred_element_type=jnp.float32) / math.sqrt(
        HEAD_SIZE
    )
    inside = valid[:, None]
    scores = jnp.where(inside, scores, NEG_FILL)
    highest = jnp.max(scores, axis=-1)
    weights = jnp.where(inside, jnp.exp(scores - highest[..., None]), 0.0).astype(jnp.bfloat16)
    totals = jnp.sum(weights.astype(jnp.float32), axis=-1)
    weighted = jnp.einsum("rkmb,rbkd->rkmd", weights, values, preferred_element_type=jnp.float32)
    return (highest, totals, weighted)


def body(q, nk, nv, kc, vc, cache_len, resid, gain, w_gate, w_up, w_down):
    steps, rows, model = q.shape
    page = kc.shape[1]
    width = w_gate.shape[0]
    units = w_gate.shape[1]
    group = QUERY_HEADS // KEY_VALUE_HEADS
    me = lax.axis_index("seq")
    positions = me * page + jnp.arange(page, dtype=jnp.int32)
    valid = (positions[None, :] < cache_len[:, None])[:, None, :]
    qv = q.reshape(steps, rows, KEY_VALUE_HEADS, group, HEAD_SIZE).transpose(1, 2, 0, 3, 4)
    qv = qv.reshape(rows, KEY_VALUE_HEADS, steps * group, HEAD_SIZE)
    keys = kc.reshape(rows, page, KEY_VALUE_HEADS, HEAD_SIZE)
    values = vc.reshape(rows, page, KEY_VALUE_HEADS, HEAD_SIZE)
    local = partial_softmax(qv, keys, values, jnp.broadcast_to(valid, (rows, steps * group, page)))
    highest = lax.pmax(local[0], "seq")
    factor = jnp.exp(local[0] - highest)
    totals, weighted = lax.psum((factor * local[1], factor[..., None] * local[2]), "seq")
    fk = jnp.swapaxes(nk, 0, 1).reshape(rows, steps, KEY_VALUE_HEADS, HEAD_SIZE)
    fv = jnp.swapaxes(nv, 0, 1).reshape(rows, steps, KEY_VALUE_HEADS, HEAD_SIZE)
    step_of = jnp.arange(steps * group, dtype=jnp.int32) // group
    causal = jnp.arange(steps, dtype=jnp.int32)[None, :] <= step_of[:, None]
    fresh = partial_softmax(
        qv, fk, fv, jnp.broadcast_to(causal[None], (rows, steps * group, steps))
    )
    peak = jnp.maximum(highest, fresh[0])
    a = jnp.exp(highest - peak)
    b = jnp.exp(fresh[0] - peak)
    total = a * totals + b * fresh[1]
    acc = a[..., None] * weighted + b[..., None] * fresh[2]
    attn = (acc / total[..., None]).astype(jnp.bfloat16)
    attn = attn.reshape(rows, KEY_VALUE_HEADS, steps, group, HEAD_SIZE).transpose(2, 0, 1, 3, 4)
    attn = attn.reshape(steps, rows, model)
    attn = lax.optimization_barrier(attn).astype(jnp.float32)
    stream = (resid.astype(jnp.float32) + attn).astype(jnp.bfloat16)
    stream = lax.optimization_barrier(stream).astype(jnp.float32)
    scaled = lax.rsqrt(jnp.mean(stream * stream, axis=-1, keepdims=True) + EPSILON)
    normed = (stream * scaled * gain.astype(jnp.float32)).astype(jnp.bfloat16)
    own = lax.dynamic_slice_in_dim(normed, me * width, width, 2)
    every = lax.all_gather(own, "req", axis=1, tiled=True).reshape(-1, width)
    joined = jnp.concatenate([w_gate, w_up], axis=1)
    sums = lax.psum(jnp.dot(every, joined, preferred_element_type=jnp.float32), "seq")
    hidden = (jax.nn.silu(sums[:, :units]) * sums[:, units:]).astype(jnp.bfloat16)
    down = jnp.dot(hidden, w_down, preferred_element_type=jnp.float32)
    down = lax.psum_scatter(down.reshape(steps, -1, width), "req", scatter_dimension=1, tiled=True)
    piece = (lax.dynamic_slice_in_dim(stream, me * width, width, 2) + down).astype(jnp.bfloat16)
    return lax.all_gather(piece, "seq", axis=2, tiled=True)


def solution(mesh):
    placed = (
        P(None, "req", None),
        P(None, "req", None),
        P(None, "req", None),
        P("req", "seq", None),
        P("req", "seq", None),
        P("req"),
        P(None, "req", None),
        P(),
        P("seq", "req"),
        P("seq", "req"),
        P("req", "seq"),
    )
    return jax.shard_map(
        body, mesh=mesh, in_specs=placed, out_specs=P(None, "req", None), check_vma=False
    )
```

profile of v0, /device:TPU:8, one launch (start us, length us, event | category | flops | bytes accessed | tf_op | source)
XLA Modules:
  0.0 988.8 jit_solution(13132273959055247014)
XLA Ops:
  6.5 0.0 copy-start
  6.5 0.0 all-reduce.4.cloned.1.call-start
  6.5 0.0 copy-start.4
  6.6 1.1 copy.49
  7.6 0.7 broadcast_compare_fusion
  8.4 1.5 fusion.27
  9.8 0.0 copy-start.5
  9.9 261.8 %pmax.7 = f32[8,8,8]{2,1,0:T(8,128)S(1)} all-reduce(f32[8,8,8]{2,1,0:T(8,128)S(1)} %get-tuple-element.10), channel_id=1, replica_groups=mesh['seq'=64,'req'=8] {'seq'}, use_global_device_ids=true, to_apply=%region_1.2 | all-reduce | flops 512 | bytes 4096 | tf_op jit(solution)/shard_map/pmax | solution.py:41
  271.6 0.3 convert_reduce_fusion
  271.9 0.0 copy-done
  271.9 1.0 convolution_multiply_fusion.1
  272.9 0.0 all-reduce.4.cloned.1.call-update
  273.0 0.0 all-reduce.6.cloned.1.call-start
  273.0 0.0 copy-done.4
  273.1 0.0 copy-start.1
  273.1 0.2 fusion.28
  273.3 0.1 convert_reduce_fusion.1
  273.4 0.8 dynamic-slice.2
  274.2 274.0 %psum.22 = f32[8,8,8]{2,1,0:T(8,128)S(1)} all-reduce(f32[8,8,8]{2,1,0:T(8,128)S(1)} %get-tuple-element.8), channel_id=1, replica_groups=mesh['seq'=64,'req'=8] {'seq'}, use_global_device_ids=true, to_apply=%region_5.6 | all-reduce | flops 512 | bytes 4096 | tf_op jit(solution)/shard_map/psum | solution.py:43
  548.3 0.0 all-reduce.4.cloned.1.call-done
  548.3 0.0 copy-done.5
  548.3 0.0 copy-start.2
  548.3 0.0 copy-start.3
  548.3 1.4 fusion.3
  549.7 0.2 copy.54
  549.9 0.0 copy-done.1
  549.9 0.1 multiply_reduce_fusion
  550.1 0.1 multiply_convert_fusion
  550.2 13.1 %all_gather.6 = bf16[4,64,32]{2,0,1:T(4,128)(2,1)S(1)} all-gather(bf16[4,8,32]{2,0,1:T(4,128)(2,1)S(1)} %copy.55), channel_id=1, replica_groups=mesh['seq'=64,'req'=8] {'req'}, dimensions={1}, use_global_device_ids=true | all-gather | bytes 18432 | tf_op jit(solution)/shard_map/all_gather | solution.py:65
  563.2 0.1 copy.56
  563.3 0.1 reshape.71
  563.4 0.0 copy-done.2
  563.4 0.0 copy-done.3
  563.4 0.0 copy-start.6
  563.5 1.5 fusion.12
  565.0 0.0 all-reduce.6.cloned.1.call-update
  565.0 1.3 dynamic-slice
  566.9 286.0 %all-reduce.6.cloned.1.call-done = f32[256,1536]{1,0:T(8,128)} async-done(((f32[256,1536]{1,0:T(8,128)}), f32[256,1536]{1,0:T(8,128)}) %all-reduce.6.cloned.1.call-update) | async-done | bytes 1572880 | tf_op jit(solution)/shard_map/psum | solution.py:67
  852.9 0.0 copy-done.6
  852.9 1.7 fusion.10
  854.6 0.1 reshape.72
  854.7 0.1 copy.57
  854.9 24.7 %all-reduce = f32[4,64,32]{2,0,1:T(4,128)S(1)} all-reduce(f32[4,64,32]{2,0,1:T(4,128)S(1)} %copy.57), channel_id=2, replica_groups=mesh['seq'=64,'req'=8] {'req'}, use_global_device_ids=true, to_apply=%region_9.10.clone | all-reduce | flops 8192 | bytes 65536
  879.6 0.1 fusion.20
  879.7 0.1 copy.59
  879.8 100.1 %all_gather.7 = bf16[4,8,2048]{1,0,2:T(4,128)(2,1)S(1)} all-gather(bf16[4,8,32]{1,0,2:T(4,128)(2,1)S(1)} %copy.59), channel_id=1, replica_groups=mesh['seq'=64,'req'=8] {'seq'}, dimensions={2}, use_global_device_ids=true | all-gather | bytes 133120 | tf_op jit(solution)/shard_map/all_gather | solution.py:72
  979.9 2.1 copy.60
  (10 shorter events, 0.1 us)
Async XLA Ops:
  6.5 265.4 %copy-start = (bf16[8,32,1024]{2,1,0:T(8,128)(2,1)S(1)}, bf16[8,32,1024]{2,1,0:T(8,128)(2,1)}, u32[]{:S(2)}) copy-start(bf16[8,32,1024]{2,1,0:T(8,128)(2,1)} %param.15) | copy-start | bytes 1572868
  6.5 541.8 %all-reduce.4.cloned.1.call-start = ((), (), s32[]{:S(2)}) async-start(), calls=%async_computation | async-start | bytes 524288 | tf_op jit(solution)/shard_map/psum | solution.py:43
  6.5 266.5 %copy-start.4 = (bf16[4,8,1024]{2,1,0:T(8,128)(2,1)S(1)}, bf16[4,8,1024]{2,1,0:T(8,128)(2,1)}, u32[]{:S(2)}) copy-start(bf16[4,8,1024]{2,1,0:T(8,128)(2,1)} %param.12) | copy-start | bytes 196612
  9.8 538.5 %copy-start.5 = (bf16[4,8,1024]{2,1,0:T(8,128)(2,1)S(1)}, bf16[4,8,1024]{2,1,0:T(8,128)(2,1)}, u32[]{:S(2)}) copy-start(bf16[4,8,1024]{2,1,0:T(8,128)(2,1)} %param.13) | copy-start | bytes 196612
  273.0 579.9 %all-reduce.6.cloned.1.call-start = ((), (), s32[]{:S(2)}) async-start(), calls=%async_computation.1 | async-start | bytes 3145728 | tf_op jit(solution)/shard_map/psum | solution.py:67
  273.1 276.8 %copy-start.1 = (bf16[4,8,2048]{2,1,0:T(8,128)(2,1)S(1)}, bf16[4,8,2048]{2,1,0:T(8,128)(2,1)}, u32[]{:S(2)}) copy-start(bf16[4,8,2048]{2,1,0:T(8,128)(2,1)} %param.17) | copy-start | bytes 393220
  548.3 15.1 %copy-start.2 = (bf16[32,768]{1,0:T(8,128)(2,1)S(1)}, bf16[32,768]{1,0:T(8,128)(2,1)}, u32[]{:S(2)}) copy-start(bf16[32,768]{1,0:T(8,128)(2,1)} %param.20) | copy-start | bytes 147460
  548.3 15.1 %copy-start.3 = (bf16[32,768]{1,0:T(8,128)(2,1)S(1)}, bf16[32,768]{1,0:T(8,128)(2,1)}, u32[]{:S(2)}) copy-start(bf16[32,768]{1,0:T(8,128)(2,1)} %param.19) | copy-start | bytes 147460
  563.4 289.5 %copy-start.6 = (bf16[768,32]{0,1:T(8,128)(2,1)S(1)}, bf16[768,32]{0,1:T(8,128)(2,1)}, u32[]{:S(2)}) copy-start(bf16[768,32]{0,1:T(8,128)(2,1)} %param.21) | copy-start | bytes 147460
Sparse Core Ops, SparseCore 0:
  273.1 274.0 all-reduce.3
  565.1 287.7 all-reduce.5
where the time goes:
time: 989 us
  blocking collectives  674 us (68%)
  waiting for transfers between devices  286 us (29%)
  between operations  14.3 us (1%)
    psum x1, waiting for transfers between devices, body(): lax.psum(jnp.dot(every, joined, preferred_element_type=jnp.float32), 'seq')  286 us
    psum x1, blocking collectives, body(): lax.psum((factor * local[1], factor[..., None] * local[2]), 'seq')  274 us
    pmax x1, blocking collectives, body(): highest = lax.pmax(local[0], 'seq')  262 us
    all_gather x1, blocking collectives, body(): return lax.all_gather(piece, 'seq', axis=2, tiled=True)  100 us
    unnamed x1, blocking collectives  24.7 us
  transfers between devices with their start and end apart: 2, of which 1 were waited for; matrix products, arithmetic and copies ran while one was open for 0% of the time, Pallas kernels for 0%

commit v1 on v0

--- a/solution.py
+++ b/solution.py
@@ -9,6 +9,12 @@
 HEAD_SIZE = 128
 NEG_FILL = -1e30
 EPSILON = 1e-06
+
+
+def handle_meshes(axis_tag, panel):
+    a_now = jnp.concatenate(lax.axis_size(axis_tag) * [panel], axis=2)
+    long_array = lax.all_to_all(a_now, axis_tag, 2, 2, tiled=True)
+    return long_array
 
 
 def partial_softmax(q, keys, values, valid):
@@ -69,7 +75,7 @@
     down = jnp.dot(hidden, w_down, preferred_element_type=jnp.float32)
     down = lax.psum_scatter(down.reshape(steps, -1, width), "req", scatter_dimension=1, tiled=True)
     piece = (lax.dynamic_slice_in_dim(stream, me * width, width, 2) + down).astype(jnp.bfloat16)
-    return lax.all_gather(piece, "seq", axis=2, tiled=True)
+    return handle_meshes("seq", piece)
 
 
 def solution(mesh):

time: 989 us -> 920 us (0.930)
  blocking collectives: 674 us -> 598 us
    all_gather x1 -> x0, blocking collectives: 100 us -> none  [body(): return lax.all_gather(piece, 'seq', axis=2, tiled=True)]
    all_to_all x0 -> x1, blocking collectives: none -> 24.5 us  [handle_meshes(): long_array = lax.all_to_all(a_now, axis_tag, 2, 2, tiled=True)]
where the time goes in v1:
time: 920 us
  blocking collectives  598 us (65%)
  waiting for transfers between devices  286 us (31%)
  between operations  14.3 us (2%)
  local copies, waits for them, and re-layouts  12.2 us (1%)
    psum x1, waiting for transfers between devices, body(): lax.psum(jnp.dot(every, joined, preferred_element_type=jnp.float32), 'seq')  286 us
    psum x1, blocking collectives, body(): lax.psum((factor * local[1], factor[..., None] * local[2]), 'seq')  274 us
    pmax x1, blocking collectives, body(): highest = lax.pmax(local[0], 'seq')  262 us
    unnamed x1, blocking collectives  24.7 us
    all_to_all x1, blocking collectives, handle_meshes(): long_array = lax.all_to_all(a_now, axis_tag, 2, 2, tiled=True)  24.5 us
  transfers between devices with their start and end apart: 2, of which 1 were waited for; matrix products, arithmetic and copies ran while one was open for 0% of the time, Pallas kernels for 0%

profile of v1, /device:TPU:8, one launch (start us, length us, event | category | flops | bytes accessed | tf_op | source)
XLA Modules:
  0.0 919.6 jit_solution(11777728891706719285)
XLA Ops:
  6.5 0.0 copy-start
  6.5 0.0 all-reduce.4.cloned.1.call-start
  6.6 1.1 copy.123
  7.6 0.7 broadcast_compare_fusion
  8.4 1.5 fusion.27
  9.9 261.8 %pmax.7 = f32[8,8,8]{2,1,0:T(8,128)S(1)} all-reduce(f32[8,8,8]{2,1,0:T(8,128)S(1)} %get-tuple-element.10), channel_id=1, replica_groups=mesh['seq'=64,'req'=8] {'seq'}, use_global_device_ids=true, to_apply=%region_1.2 | all-reduce | flops 512 | bytes 4096 | tf_op jit(solution)/shard_map/pmax | solution.py:47
  271.6 0.3 convert_reduce_fusion
  271.9 0.0 copy-done
  271.9 1.0 convolution_multiply_fusion.1
  272.9 0.0 all-reduce.4.cloned.1.call-update
  273.0 0.0 all-reduce.6.cloned.1.call-start
  273.0 0.0 copy-done.4
  273.1 0.0 copy-start.1
  273.1 0.2 fusion.28
  273.3 0.1 convert_reduce_fusion.1
  273.4 0.8 dynamic-slice.2
  274.2 274.0 %psum.22 = f32[8,8,8]{2,1,0:T(8,128)S(1)} all-reduce(f32[8,8,8]{2,1,0:T(8,128)S(1)} %get-tuple-element.8), channel_id=1, replica_groups=mesh['seq'=64,'req'=8] {'seq'}, use_global_device_ids=true, to_apply=%region_5.6 | all-reduce | flops 512 | bytes 4096 | tf_op jit(solution)/shard_map/psum | solution.py:49
  548.3 0.0 all-reduce.4.cloned.1.call-done
  548.3 0.0 copy-done.5
  548.3 0.0 copy-start.2
  548.3 0.0 copy-start.3
  548.3 1.4 fusion.3
  549.7 0.2 copy.128
  549.9 0.0 copy-done.1
  549.9 0.1 multiply_reduce_fusion
  550.1 0.1 multiply_convert_fusion
  550.2 13.0 %all_gather.3 = bf16[4,64,32]{2,0,1:T(4,128)(2,1)S(1)} all-gather(bf16[4,8,32]{2,0,1:T(4,128)(2,1)S(1)} %copy.129), channel_id=1, replica_groups=mesh['seq'=64,'req'=8] {'req'}, dimensions={1}, use_global_device_ids=true | all-gather | bytes 18432 | tf_op jit(solution)/shard_map/all_gather | solution.py:71
  563.2 0.1 copy.130
  563.3 0.1 reshape.71
  563.4 0.0 copy-done.2
  563.4 0.0 copy-done.3
  563.4 0.0 copy-start.6
  563.5 1.5 fusion.12
  565.0 0.0 all-reduce.6.cloned.1.call-update
  565.0 1.3 dynamic-slice
  566.9 286.0 %all-reduce.6.cloned.1.call-done = f32[256,1536]{1,0:T(8,128)} async-done(((f32[256,1536]{1,0:T(8,128)}), f32[256,1536]{1,0:T(8,128)}) %all-reduce.6.cloned.1.call-update) | async-done | bytes 1572880 | tf_op jit(solution)/shard_map/psum | solution.py:73
  853.0 0.0 copy-done.6
  853.0 1.7 fusion.10
  854.7 0.1 reshape.72
  854.8 0.1 copy.131
  854.9 24.7 %all-reduce = f32[4,64,32]{2,0,1:T(4,128)S(1)} all-reduce(f32[4,64,32]{2,0,1:T(4,128)S(1)} %copy.131), channel_id=2, replica_groups=mesh['seq'=64,'req'=8] {'req'}, use_global_device_ids=true, to_apply=%region_9.10.clone | all-reduce | flops 8192 | bytes 65536
  879.6 0.1 fusion.20
  879.7 0.3 concatenate.7
  880.1 1.3 copy.133
  881.4 2.3 reshape.74
  883.7 24.5 %all_to_all.5 = bf16[64,2,512]{2,1,0:T(2,128)(2,1)S(1)} all-to-all(bf16[64,2,512]{2,1,0:T(2,128)(2,1)S(1)} %reshape.74), channel_id=1, replica_groups=mesh['seq'=64,'req'=8] {'seq'}, dimensions={0} | all-to-all | bytes 262144 | tf_op jit(solution)/shard_map/all_to_all | solution.py:16
  908.2 2.4 reshape.75
  910.6 2.1 copy.134
  (12 shorter events, 0.1 us)
Async XLA Ops:
  6.5 265.4 %copy-start = (bf16[8,32,1024]{2,1,0:T(8,128)(2,1)S(1)}, bf16[8,32,1024]{2,1,0:T(8,128)(2,1)}, u32[]{:S(2)}) copy-start(bf16[8,32,1024]{2,1,0:T(8,128)(2,1)} %param.15) | copy-start | bytes 1572868
  6.5 541.8 %all-reduce.4.cloned.1.call-start = ((), (), s32[]{:S(2)}) async-start(), calls=%async_computation.1 | async-start | bytes 524288 | tf_op jit(solution)/shard_map/psum | solution.py:49
  6.5 266.5 %copy-start.4 = (bf16[4,8,1024]{2,1,0:T(8,128)(2,1)S(1)}, bf16[4,8,1024]{2,1,0:T(8,128)(2,1)}, u32[]{:S(2)}) copy-start(bf16[4,8,1024]{2,1,0:T(8,128)(2,1)} %param.12) | copy-start | bytes 196612
  9.8 538.5 %copy-start.5 = (bf16[4,8,1024]{2,1,0:T(8,128)(2,1)S(1)}, bf16[4,8,1024]{2,1,0:T(8,128)(2,1)}, u32[]{:S(2)}) copy-start(bf16[4,8,1024]{2,1,0:T(8,128)(2,1)} %param.13) | copy-start | bytes 196612
  273.0 580.0 %all-reduce.6.cloned.1.call-start = ((), (), s32[]{:S(2)}) async-start(), calls=%async_computation.2 | async-start | bytes 3145728 | tf_op jit(solution)/shard_map/psum | solution.py:73
  273.1 276.8 %copy-start.1 = (bf16[4,8,2048]{2,1,0:T(8,128)(2,1)S(1)}, bf16[4,8,2048]{2,1,0:T(8,128)(2,1)}, u32[]{:S(2)}) copy-start(bf16[4,8,2048]{2,1,0:T(8,128)(2,1)} %param.17) | copy-start | bytes 393220
  548.3 15.1 %copy-start.2 = (bf16[32,768]{1,0:T(8,128)(2,1)S(1)}, bf16[32,768]{1,0:T(8,128)(2,1)}, u32[]{:S(2)}) copy-start(bf16[32,768]{1,0:T(8,128)(2,1)} %param.20) | copy-start | bytes 147460
  548.3 15.1 %copy-start.3 = (bf16[32,768]{1,0:T(8,128)(2,1)S(1)}, bf16[32,768]{1,0:T(8,128)(2,1)}, u32[]{:S(2)}) copy-start(bf16[32,768]{1,0:T(8,128)(2,1)} %param.19) | copy-start | bytes 147460
  563.4 289.5 %copy-start.6 = (bf16[768,32]{0,1:T(8,128)(2,1)S(1)}, bf16[768,32]{0,1:T(8,128)(2,1)}, u32[]{:S(2)}) copy-start(bf16[768,32]{0,1:T(8,128)(2,1)} %param.21) | copy-start | bytes 147460
Sparse Core Ops, SparseCore 0:
  273.1 274.0 all-reduce.3
  565.1 287.7 all-reduce.5
